TPU v7x, 32 devices: a whole 2x2x4 slice. The times are simulated.
32 devices in a mesh: gx: 4 (over y, x), gy: 8 (over z, core).
Axes of the slice: x: 2, y: 2, z: 4, core: 2. Of those that a mesh axis runs over, the one named last changes fastest.
Arguments:
- old_state: float32 [8, 8, 128, 1024], P(None, None, 'gx', 'gy'), may hold values from -6 to 6
- section_prims: float32 [8, 8, 128, 1024], P(None, None, 'gx', 'gy'), may hold values from -3 to 3, as said below
- shear_whole: int32 [1], replicated, may hold values from 0 to 1023
- shear_frac: float32 [1], replicated, may hold values from 0 to 1
Outputs:
- new_state: float32 [8, 8, 128, 1024], P(None, None, 'gx', 'gy')
Inputs may be any that keep to these rules, and one draw needn't show every extreme that they name: section_prims holds density in [0.5, 2] in field 0 and pressure in [0.3, 3] in field 4; the other fields lie in the stated range.
All inputs are finite; a program needn't handle non-finite values.
Results may differ from a plain program's by a relative error of at most 0.0003.
Values sent between devices are 32-bit elements; how exact they have to be, the bound alone decides.
No kernel may reach another device: no remote copies, remote signals or barrier semaphores. Data moves between devices by JAX's collectives and lax.ppermute only.
A program may use at most 128 MiB of HBM per device.

v0:
```python
import jax
import jax.numpy as jnp
from jax import lax
from jax.sharding import PartitionSpec as P

gamma_gas = 5.0 / 3.0
omega_rate = 1.0
shear_rate = 1.5
time_step = 0.1


def with_halo(shard, sides, width):
    for axis, dim in sides:
        size, length = (lax.axis_size(axis), shard.shape[dim])
        up = [(i, (i + 1) % size) for i in range(size)]
        down = [(j, i) for i, j in up]
        last = lax.slice_in_dim(shard, length - width, length, axis=dim)
        first = lax.slice_in_dim(shard, 0, width, axis=dim)
        before = lax.ppermute(last, axis, up)
        after = lax.ppermute(first, axis, down)
        shard = jnp.concatenate([before, shard, after], axis=dim)
    return shard


def conserved(prims):
    rho = prims[0]
    kinetic = 0.5 * rho * (prims[1] * prims[1] + prims[2] * prims[2] + prims[3] * prims[3])
    magnetic = 0.5 * (prims[5] * prims[5] + prims[6] * prims[6] + prims[7] * prims[7])
    energy = prims[4] / (gamma_gas - 1.0) + kinetic + magnetic
    return jnp.stack(
        [rho, rho * prims[1], rho * prims[2], rho * prims[3], energy, prims[5], prims[6], prims[7]]
    )


def fluxes(prims, cons, direction):
    rho = prims[0]
    normal_vel = prims[1 + direction]
    normal_mag = prims[5 + direction]
    ptotal = prims[4] + 0.5 * (prims[5] * prims[5] + prims[6] * prims[6] + prims[7] * prims[7])
    vdotb = prims[1] * prims[5] + prims[2] * prims[6] + prims[3] * prims[7]
    parts = [rho * normal_vel]
    for comp in range(3):
        parts.append(rho * prims[1 + comp] * normal_vel - prims[5 + comp] * normal_mag)
    parts[1 + direction] = parts[1 + direction] + ptotal
    parts.append((cons[4] + ptotal) * normal_vel - normal_mag * vdotb)
    for comp in range(3):
        parts.append(prims[5 + comp] * normal_vel - prims[1 + comp] * normal_mag)
    return jnp.stack(parts)


def fast_speed(prims, direction):
    rho = prims[0]
    sound = gamma_gas * prims[4] / rho
    squares = [prims[5] * prims[5], prims[6] * prims[6], prims[7] * prims[7]]
    alfven = (squares[0] + squares[1] + squares[2]) / rho
    others = [squares[c] for c in range(3) if c != direction]
    transverse = (others[0] + others[1]) / rho
    disc = jnp.square(sound - alfven) + 4.0 * sound * transverse
    return jnp.sqrt(0.5 * (sound + alfven + jnp.sqrt(disc)))


def minmod(first, second):
    return 0.5 * (jnp.sign(first) + jnp.sign(second)) * jnp.minimum(jnp.abs(first), jnp.abs(second))


def rusanov(left, right, direction):
    cons_left = conserved(left)
    cons_right = conserved(right)
    flux_left = fluxes(left, cons_left, direction)
    flux_right = fluxes(right, cons_right, direction)
    speed_left = jnp.abs(left[1 + direction]) + fast_speed(left, direction)
    speed_right = jnp.abs(right[1 + direction]) + fast_speed(right, direction)
    speed = jnp.maximum(speed_left, speed_right)
    return 0.5 * (flux_left + flux_right) - 0.5 * speed * (cons_right - cons_left)


def sweep(padded, axis, direction):
    length = padded.shape[axis]
    cells = length - 4

    def take(arr, start, stop):
        return lax.slice_in_dim(arr, start, stop, axis=axis)

    diff = take(padded, 1, length) - take(padded, 0, length - 1)
    slope = minmod(take(diff, 0, length - 2), take(diff, 1, length - 1))
    left = take(padded, 1, length - 2) + 0.5 * take(slope, 0, length - 3)
    right = take(padded, 2, length - 1) - 0.5 * take(slope, 1, length - 2)
    face = rusanov(left, right, direction)
    return take(face, 1, cells + 1) - take(face, 0, cells)


def sources(core):
    rho = core[0]
    zeros = jnp.zeros_like(rho)
    return jnp.stack(
        [
            zeros,
            2.0 * omega_rate * rho * core[2],
            -(2.0 - shear_rate) * omega_rate * rho * core[1],
            zeros,
            shear_rate * omega_rate * (rho * core[1] * core[2] - core[5] * core[6]),
            zeros,
            -shear_rate * omega_rate * core[5],
            zeros,
        ]
    )


def section_update(radial_rows, azimuthal_rows, old):
    core = azimuthal_rows[:, :, :, 2:-2]
    radial = sweep(radial_rows, 2, 0)
    azimuthal = sweep(azimuthal_rows, 3, 1)
    zpadded = jnp.concatenate([core[:, -2:], core, core[:, :2]], axis=1)
    vertical = sweep(zpadded, 1, 2)
    rates = -(radial + azimuthal + vertical) + sources(core)
    return 0.5 * old + 0.5 * (conserved(core) + time_step * rates)


def on_device(old_state, section_prims, shear_whole, shear_frac):
    padded = with_halo(section_prims, (("gx", 2), ("gy", 3)), 2)
    cells = section_prims.shape[3]
    loop_size = lax.axis_size("gy")
    total = cells * loop_size
    shift_cells = shear_whole[0]
    frac = shear_frac[0]
    back_cells = (total - 1 - shift_cells) % total
    inner_src = padded[:, :, 0:2, 2:-2]
    outer_src = padded[:, :, -2:, 2:-2]
    inner_cycle, outer_cycle = (
        lax.all_gather(inner_src, "gy", axis=3, tiled=True),
        lax.all_gather(outer_src, "gy", axis=3, tiled=True),
    )
    position = lax.axis_index("gy") * cells
    inner_ext = jnp.concatenate([inner_cycle, inner_cycle[..., : cells + 1]], axis=3)
    outer_ext = jnp.concatenate([outer_cycle, outer_cycle[..., : cells + 1]], axis=3)
    inner_win = lax.dynamic_slice_in_dim(inner_ext, (position + shift_cells) % total, cells + 1, 3)
    outer_win = lax.dynamic_slice_in_dim(outer_ext, (position + back_cells) % total, cells + 1, 3)
    inner_ghost = (1.0 - frac) * inner_win[..., :cells] + frac * inner_win[..., 1:]
    outer_ghost = (1.0 - frac) * outer_win[..., 1:] + frac * outer_win[..., :cells]
    radial_index = lax.axis_index("gx")
    left_rows = jnp.where(radial_index == 0, inner_ghost, inner_src)
    right_rows = jnp.where(radial_index == lax.axis_size("gx") - 1, outer_ghost, outer_src)
    azimuthal_rows = padded[:, :, 2:-2, :]
    radial_rows = jnp.concatenate([left_rows, azimuthal_rows[:, :, :, 2:-2], right_rows], axis=2)
    return section_update(radial_rows, azimuthal_rows, old_state)


def solution(mesh):
    in_specs = (P(None, None, "gx", "gy"), P(None, None, "gx", "gy"), P(), P())
    out_specs = P(None, None, "gx", "gy")
    return jax.shard_map(
        on_device, mesh=mesh, in_specs=in_specs, out_specs=out_specs, check_vma=False
    )
```

profile of v0, /device:TPU:0, one launch (start us, length us, event | category | flops | bytes accessed | tf_op | source)
XLA Modules:
  0.0 111.1 jit_solution(10720879476394507808)
XLA Ops:
  0.0 1.9 %copy.188 = f32[8,8,32,128]{3,1,2,0:T(8,128)S(1)} copy(f32[8,8,32,128]{3,2,1,0:T(8,128)} %param.5) | data formatting | bytes 2097152 | tf_op args[1]
  1.9 1.0 copy-done.4
  3.6 3.9 %collective-permute-start.1 = (f32[8,8,2,128]{3,1,2,0:T(8,128)}, f32[8,8,2,128]{3,1,2,0:T(8,128)S(1)}, u32[]{:S(2)}, u32[]{:S(2)}) collective-permute-start(f32[8,8,2,128]{3,1,2,0:T(8,128)} %get-tuple-element.78), channel_id=1, source_target_pairs={{8,0},{16,8},{24,16},{0,24},{9,1},{17,9},{25,17},{1,25},{10,2},{18... | collective-permute-start | bytes 196616 | tf_op jit(solution)/shard_map/ppermute | solution.py:20
  8.4 1.7 %pad_maximum_fusion.5 = (f32[8,9,32,128]{3,2,1,0:T(8,128)}, f32[8,9,32,128]{3,2,1,0:T(8,128)}) fusion(f32[8,8,32,128]{3,2,1,0:T(8,128)S(1)} %copy-done.1, f32[8,2,32,128]{3,2,1,0:T(8,128)S(1)} %get-tuple-element.82, f32[8,2,32,128]{3,2,1,0:T(8,128)S(1)} %get-tuple-element.83), kind=kLoop, calls=%fused_computation.19 | loop fusion | flops 589824 | bytes 3932160 | tf_op jit(solution)/shard_map/concatenate | solution.py:113
  12.4 2.1 %copy_subtract_fusion = f32[8,11,32,128]{3,1,2,0:T(8,128)S(1)} fusion(f32[8,11,32,128]{3,2,1,0:T(8,128)S(1)} %get-tuple-element.51, f32[8,11,32,128]{3,2,1,0:T(8,128)S(1)} %get-tuple-element.50), kind=kLoop, calls=%fused_computation.12 | loop fusion | flops 360448 | bytes 4325376 | tf_op jit(solution)/shard_map/sub | solution.py:84
  14.5 1.5 %minimum_multiply_fusion = f32[8,10,32,128]{3,1,2,0:T(8,128)S(1)} fusion(f32[8,11,32,128]{3,1,2,0:T(8,128)S(1)} %copy_subtract_fusion), kind=kLoop, calls=%fused_computation.14 | loop fusion | flops 2621440 | bytes 3932160 | tf_op jit(solution)/shard_map/mul | solution.py:63
  16.1 2.2 %fusion.1 = (f32[8,9,32,128]{3,1,2,0:T(8,128)S(1)}, f32[8,9,32,128]{3,1,2,0:T(8,128)S(1)}) fusion(f32[8,10,32,128]{3,1,2,0:T(8,128)S(1)} %minimum_multiply_fusion, f32[8,9,32,128]{3,2,1,0:T(8,128)S(1)} %copy-done.8, f32[8,9,32,128]{3,2,1,0:T(8,128)S(1)} %copy-done.9), kind=kLoop, calls=%fused_computation.4 | loop fusion | flops 1179648 | bytes 7077888 | tf_op jit(solution)/shard_map/add | solution.py:86
  18.5 1.3 %multiply_bitcast_fusion = (f32[9,32,128]{2,0,1:T(8,128)}, f32[1,9,32,128]{3,1,2,0:T(8,128)S(1)}, f32[1,9,32,128]{3,1,2,0:T(8,128)S(1)}, f32[8,9,32,128]{3,1,2,0:T(8,128)S(1)}) fusion(f32[8,9,32,128]{3,1,2,0:T(8,128)S(1)} %get-tuple-element.49, f32[8,9,32,128]{3,1,2,0:T(8,128)S(1)} %get-tuple-element.48, ...), kind=kLoop, calls=%fused_computation.52 | loop fusion | flops 1622016 | bytes 4341760 | tf_op jit(solution)/shard_map/mul | solution.py:74
  23.6 0.9 subtract_dynamic-update-slice_fusion.9
  31.2 0.8 constant_dynamic-update-slice_fusion.59
  32.0 0.8 slice_dynamic-update-slice_fusion.6
  33.6 2.1 %constant_dynamic-update-slice_fusion.53 = f32[8,9,32,128]{3,1,2,0:T(8,128)} fusion(f32[8,9,32,128]{3,1,2,0:T(8,128)} %constant_dynamic-update-slice_fusion.54, f32[1,9,32,128]{3,1,2,0:T(8,128)} %get-tuple-element.25), kind=kLoop, calls=%fused_computation.157 | loop fusion | bytes 524288
  35.7 2.5 %slice_dynamic-update-slice_fusion = (f32[8,9,32,128]{3,1,2,0:T(8,128)}, f32[8,9,32,128]{3,1,2,0:T(8,128)}) fusion(f32[8,9,32,128]{3,1,2,0:T(8,128)} %constant_dynamic-update-slice_fusion.53, f32[8,9,32,128]{3,1,2,0:T(8,128)} %copy-done, f32[8,9,32,128]{3,1,2,0:T(8,128)} %constant_dynamic-update-slice_fusion.48, f32[8,9,32,128]{3,1,2,0:T(8,128)S(1)} %get-tuple-element.49), kind=kLoop, calls=%fused_computation.41 | loop fusion | bytes 2801664 | tf_op jit(solution)/shard_map/stack | solution.py:30
  38.2 4.1 %multiply_subtract_fusion = f32[8,9,32,128]{3,1,2,0:T(8,128)} fusion(f32[8,9,32,128]{3,1,2,0:T(8,128)} %get-tuple-element.89, f32[8,9,32,128]{3,1,2,0:T(8,128)} %get-tuple-element.88, f32[8,9,32,128]{3,1,2,0:T(8,128)S(1)} %copy-done.13, f32[8,9,32,128]{3,1,2,0:T(8,128)S(1)} %copy-done.11, f32[9,32,128]{2,0,1:T(8,128)} %get-tuple-element.19), kind=kLoop, calls=%fused_computation.13 | loop fusion | flops 1474560 | bytes 6045696 | tf_op jit(solution)/shard_map/sub | solution.py:74
  43.0 15.0 %all_gather.7 = f32[8,8,2,1024]{3,1,2,0:T(8,128)S(1)} all-gather(f32[8,8,2,128]{3,1,2,0:T(8,128)S(1)} %collective-permute-done.1), channel_id=1, replica_groups=mesh['gx'=4,'gy'=8] {'gy'}, dimensions={3}, use_global_device_ids=true | all-gather | bytes 589824 | tf_op jit(solution)/shard_map/all_gather | solution.py:131
  58.1 15.1 %all_gather.6 = f32[8,8,2,1024]{3,1,2,0:T(8,128)S(1)} all-gather(f32[8,8,2,128]{3,1,2,0:T(8,128)S(1)} %collective-permute-done), channel_id=1, replica_groups=mesh['gx'=4,'gy'=8] {'gy'}, dimensions={3}, use_global_device_ids=true | all-gather | bytes 589824 | tf_op jit(solution)/shard_map/all_gather | solution.py:130
  75.2 0.9 multiply_bitcast_fusion.2
  77.1 1.0 constant_dynamic-update-slice_fusion.8
  78.1 1.0 copy-done.16
  79.1 1.4 %fusion.21 = (f32[8,8,36,2]{3,1,2,0:T(8,128)}, f32[8,8,36,2]{3,1,2,0:T(8,128)S(1)}) fusion(f32[8,8,36,128]{3,1,2,0:T(8,128)S(1)} %get-tuple-element.87), kind=kLoop, calls=%fused_computation.205 | loop fusion | bytes 73728 | tf_op jit(solution)/shard_map/slice | solution.py:17
  80.5 1.8 %copy.194 = f32[8,8,36,2]{2,1,3,0:T(8,128)S(1)} copy(f32[8,8,36,2]{3,1,2,0:T(8,128)} %get-tuple-element.52) | data formatting | bytes 36864 | tf_op jit(solution)/shard_map/slice | solution.py:17
  82.7 1.2 %copy.196 = f32[8,8,36,2]{2,1,3,0:T(8,128)} copy(f32[8,8,36,2]{3,1,2,0:T(8,128)S(1)} %get-tuple-element.53) | data formatting | bytes 36864 | tf_op jit(solution)/shard_map/slice | solution.py:18
  83.9 3.4 %collective-permute-start.3 = (f32[8,8,36,2]{2,1,3,0:T(8,128)}, f32[8,8,36,2]{2,1,3,0:T(8,128)}, u32[]{:S(2)}, u32[]{:S(2)}) collective-permute-start(f32[8,8,36,2]{2,1,3,0:T(8,128)} %copy.196), channel_id=1, source_target_pairs={{1,0},{2,1},{3,2},{4,3},{5,4},{6,5},{7,6},{0,7},{9,8},{10,9},{11,1... | collective-permute-start | bytes 55304 | tf_op jit(solution)/shard_map/ppermute | solution.py:20
  90.4 1.1 copy-done.15
  91.8 1.2 %multiply_subtract_fusion.2 = f32[8,8,33,128]{3,1,2,0:T(8,128)} fusion(f32[8,8,33,128]{3,1,2,0:T(8,128)S(1)} %get-tuple-element.93, f32[8,8,33,128]{3,1,2,0:T(8,128)S(1)} %get-tuple-element.92, f32[8,8,33,128]{3,1,2,0:T(8,128)S(1)} %get-tuple-element.60, f32[8,8,33,128]{3,1,2,0:T(8,128)S(1)} %copy-done.19, f32[8,33,128]{2,0,1:T(8,128)S(1)} %get-tuple-element.5), kind=kLoop, calls=%fused_computation.29 | loop fusion | flops 1351680 | bytes 5541888 | tf_op jit(solution)/shard_map/sub | solution.py:74
  92.9 1.5 %copy.195 = f32[8,8,36,2]{3,1,2,0:T(8,128)S(1)} copy(f32[8,8,36,2]{2,1,3,0:T(8,128)} %collective-permute-done.2) | data formatting | bytes 36864 | tf_op jit(solution)/shard_map/ppermute | solution.py:19
  94.5 1.4 %copy.198 = f32[8,8,36,2]{3,1,2,0:T(8,128)S(1)} copy(f32[8,8,36,2]{2,1,3,0:T(8,128)} %collective-permute-done.3) | data formatting | bytes 36864 | tf_op jit(solution)/shard_map/ppermute | solution.py:20
  95.9 1.0 pad_maximum_fusion
  97.5 1.4 %minimum_multiply_fusion.1 = f32[8,8,32,130]{3,1,2,0:T(8,128)S(1)} fusion(f32[8,8,32,131]{3,1,2,0:T(8,128)S(1)} %slice_subtract_fusion), kind=kLoop, calls=%fused_computation.16 | loop fusion | flops 2129920 | bytes 3194880 | tf_op jit(solution)/shard_map/mul | solution.py:63
  99.0 1.5 %fusion.3 = (f32[8,8,32,129]{3,1,2,0:T(8,128)S(1)}, f32[8,8,32,129]{3,1,2,0:T(8,128)S(1)}) fusion(f32[8,8,32,130]{3,1,2,0:T(8,128)S(1)} %minimum_multiply_fusion.1, f32[8,8,36,128]{3,1,2,0:T(8,128)S(1)} %copy-done.3, f32[8,8,36,2]{3,1,2,0:T(8,128)S(1)} %copy.195, f32[8,8,36,2]{3,1,2,0:T(8,128)S(1)} %copy.198), kind=kLoop, calls=%fused_computation.9 | loop fusion | flops 1585152 | bytes 5443584 | tf_op jit(solution)/shard_map/add | solution.py:86
  105.1 4.8 %fusion.12 = f32[8,8,32,128]{3,1,2,0:T(8,128)S(1)} fusion(f32[8,9,32,128]{3,1,2,0:T(8,128)S(1)} %copy-done.7, f32[8,8,32,129]{3,1,2,0:T(8,128)S(1)} %multiply_subtract_fusion.1, f32[8,8,33,128]{3,1,2,0:T(8,128)S(1)} %copy-done.6, f32[8,8,32,128]{3,2,1,0:T(8,128)S(1)} %copy-done.20, f32[8,8,32,128]{3,2,1,0:T(8,128)} %slice_dynamic-update-slice_fusion.6, ...), kind=kLoop, calls=%fused_computation.37 | loop fusion | flops 2883584 | bytes 10485760 | tf_op jit(solution)/shard_map/add | solution.py:116
  109.9 1.2 %copy.207 = f32[8,8,32,128]{3,2,1,0:T(8,128)} copy(f32[8,8,32,128]{3,1,2,0:T(8,128)S(1)} %fusion.12) | data formatting | bytes 2097152 | tf_op jit(solution)/shard_map/add | solution.py:116
  (132 shorter events, 26.4 us)
Async XLA Ops:
  0.0 8.2 %copy-start.1 = (f32[8,8,32,128]{3,2,1,0:T(8,128)S(1)}, f32[8,8,32,128]{3,2,1,0:T(8,128)}, u32[]{:S(2)}) copy-start(f32[8,8,32,128]{3,2,1,0:T(8,128)} %param.5) | copy-start | bytes 3145732
  1.9 1.0 copy-start.4
  3.6 39.4 %collective-permute-start.1 = (f32[8,8,2,128]{3,1,2,0:T(8,128)}, f32[8,8,2,128]{3,1,2,0:T(8,128)S(1)}, u32[]{:S(2)}, u32[]{:S(2)}) collective-permute-start(f32[8,8,2,128]{3,1,2,0:T(8,128)} %get-tuple-element.78), channel_id=1, source_target_pairs={{8,0},{16,8},{24,16},{0,24},{9,1},{17,9},{25,17},{1,25},{10,2},{18... | collective-permute-start | bytes 196616 | tf_op jit(solution)/shard_map/ppermute | solution.py:20
  7.5 50.6 %collective-permute-start = (f32[8,8,2,128]{3,1,2,0:T(8,128)}, f32[8,8,2,128]{3,1,2,0:T(8,128)S(1)}, u32[]{:S(2)}, u32[]{:S(2)}) collective-permute-start(f32[8,8,2,128]{3,1,2,0:T(8,128)} %get-tuple-element.79), channel_id=1, source_target_pairs={{0,8},{8,16},{16,24},{24,0},{1,9},{9,17},{17,25},{25,1},{2,10},{10... | collective-permute-start | bytes 196616 | tf_op jit(solution)/shard_map/ppermute | solution.py:19
  14.5 1.5 %copy-start.8 = (f32[8,9,32,128]{3,2,1,0:T(8,128)S(1)}, f32[8,9,32,128]{3,2,1,0:T(8,128)}, u32[]{:S(2)}) copy-start(f32[8,9,32,128]{3,2,1,0:T(8,128)} %get-tuple-element.80) | copy-start | bytes 3538948
  14.5 1.6 %copy-start.9 = (f32[8,9,32,128]{3,2,1,0:T(8,128)S(1)}, f32[8,9,32,128]{3,2,1,0:T(8,128)}, u32[]{:S(2)}) copy-start(f32[8,9,32,128]{3,2,1,0:T(8,128)} %get-tuple-element.81) | copy-start | bytes 3538948
  18.3 8.5 %copy-start = (f32[8,9,32,128]{3,1,2,0:T(8,128)}, f32[8,9,32,128]{3,1,2,0:T(8,128)S(1)}, u32[]{:S(2)}) copy-start(f32[8,9,32,128]{3,1,2,0:T(8,128)S(1)} %get-tuple-element.48) | copy-start | bytes 3538948
  21.3 3.2 %copy-start.10 = (f32[8,9,32,128]{3,1,2,0:T(8,128)}, f32[8,9,32,128]{3,1,2,0:T(8,128)S(1)}, u32[]{:S(2)}) copy-start(f32[8,9,32,128]{3,1,2,0:T(8,128)S(1)} %get-tuple-element.43) | copy-start | bytes 3538948
  25.4 5.2 %copy-start.12 = (f32[8,9,32,128]{3,1,2,0:T(8,128)}, f32[8,9,32,128]{3,1,2,0:T(8,128)S(1)}, u32[]{:S(2)}) copy-start(f32[8,9,32,128]{3,1,2,0:T(8,128)S(1)} %get-tuple-element.45) | copy-start | bytes 3538948
  32.9 5.4 %copy-start.11 = (f32[8,9,32,128]{3,1,2,0:T(8,128)S(1)}, f32[8,9,32,128]{3,1,2,0:T(8,128)}, u32[]{:S(2)}) copy-start(f32[8,9,32,128]{3,1,2,0:T(8,128)} %copy-done.10) | copy-start | bytes 3538948
  32.9 5.4 %copy-start.13 = (f32[8,9,32,128]{3,1,2,0:T(8,128)S(1)}, f32[8,9,32,128]{3,1,2,0:T(8,128)}, u32[]{:S(2)}) copy-start(f32[8,9,32,128]{3,1,2,0:T(8,128)} %copy-done.12) | copy-start | bytes 3538948
  73.2 1.2 %copy-start.5 = (f32[8,8,32,128]{3,1,2,0:T(8,128)S(1)}, f32[8,8,32,128]{3,1,2,0:T(8,128)}, u32[]{:S(2)}) copy-start(f32[8,8,32,128]{3,1,2,0:T(8,128)} %copy-done.4) | copy-start | bytes 3145732
  74.3 4.8 %copy-start.2 = (f32[8,8,36,128]{3,1,2,0:T(8,128)}, f32[8,8,36,128]{3,1,2,0:T(8,128)S(1)}, u32[]{:S(2)}) copy-start(f32[8,8,36,128]{3,1,2,0:T(8,128)S(1)} %get-tuple-element.87) | copy-start | bytes 3538948
  76.9 1.2 %copy-start.18 = (f32[8,8,33,128]{3,1,2,0:T(8,128)}, f32[8,8,33,128]{3,1,2,0:T(8,128)S(1)}, u32[]{:S(2)}) copy-start(f32[8,8,33,128]{3,1,2,0:T(8,128)S(1)} %get-tuple-element.8) | copy-start | bytes 3244036
  78.1 1.0 copy-start.16
  82.3 10.7 %collective-permute-start.2 = (f32[8,8,36,2]{2,1,3,0:T(8,128)S(1)}, f32[8,8,36,2]{2,1,3,0:T(8,128)}, u32[]{:S(2)}, u32[]{:S(2)}) collective-permute-start(f32[8,8,36,2]{2,1,3,0:T(8,128)S(1)} %copy.194), channel_id=1, source_target_pairs={{0,1},{1,2},{2,3},{3,4},{4,5},{5,6},{6,7},{7,0},{8,9},{9,10},{10,1... | collective-permute-start | bytes 55304 | tf_op jit(solution)/shard_map/ppermute | solution.py:19
  83.9 5.6 %copy-start.22 = (f32[1,8,33,128]{3,1,2,0:T(8,128)S(1)}, f32[1,8,33,128]{3,1,2,0:T(8,128)}, u32[]{:S(2)}) copy-start(f32[1,8,33,128]{3,1,2,0:T(8,128)} %get-tuple-element.9) | copy-start | bytes 405508
  83.9 6.3 %copy-start.14 = (f32[8,8,33,128]{3,1,2,0:T(8,128)S(1)}, f32[8,8,33,128]{3,1,2,0:T(8,128)}, u32[]{:S(2)}) copy-start(f32[8,8,33,128]{3,1,2,0:T(8,128)} %get-tuple-element.66) | copy-start | bytes 3244036
  83.9 6.3 %copy-start.17 = (f32[8,8,33,128]{3,1,2,0:T(8,128)S(1)}, f32[8,8,33,128]{3,1,2,0:T(8,128)}, u32[]{:S(2)}) copy-start(f32[8,8,33,128]{3,1,2,0:T(8,128)} %copy-done.16) | copy-start | bytes 3244036
  83.9 10.6 %collective-permute-start.3 = (f32[8,8,36,2]{2,1,3,0:T(8,128)}, f32[8,8,36,2]{2,1,3,0:T(8,128)}, u32[]{:S(2)}, u32[]{:S(2)}) collective-permute-start(f32[8,8,36,2]{2,1,3,0:T(8,128)} %copy.196), channel_id=1, source_target_pairs={{1,0},{2,1},{3,2},{4,3},{5,4},{6,5},{7,6},{0,7},{9,8},{10,9},{11,1... | collective-permute-start | bytes 55304 | tf_op jit(solution)/shard_map/ppermute | solution.py:20
  88.8 1.6 %copy-start.21 = (f32[1,8,33,128]{3,1,2,0:T(8,128)S(1)}, f32[1,8,33,128]{3,1,2,0:T(8,128)}, u32[]{:S(2)}) copy-start(f32[1,8,33,128]{3,1,2,0:T(8,128)} %get-tuple-element.11) | copy-start | bytes 405508
  90.2 1.2 %copy-start.15 = (f32[8,8,33,128]{3,1,2,0:T(8,128)S(1)}, f32[8,8,33,128]{3,1,2,0:T(8,128)}, u32[]{:S(2)}) copy-start(f32[8,8,33,128]{3,1,2,0:T(8,128)} %constant_dynamic-update-slice_fusion.21) | copy-start | bytes 3244036
  90.2 1.6 %copy-start.19 = (f32[8,8,33,128]{3,1,2,0:T(8,128)S(1)}, f32[8,8,33,128]{3,1,2,0:T(8,128)}, u32[]{:S(2)}) copy-start(f32[8,8,33,128]{3,1,2,0:T(8,128)} %get-tuple-element.54) | copy-start | bytes 3244036
  92.9 2.9 %copy-start.3 = (f32[8,8,36,128]{3,1,2,0:T(8,128)S(1)}, f32[8,8,36,128]{3,1,2,0:T(8,128)}, u32[]{:S(2)}) copy-start(f32[8,8,36,128]{3,1,2,0:T(8,128)} %copy-done.2) | copy-start | bytes 3538948
  102.9 1.2 %copy-start.6 = (f32[8,8,33,128]{3,1,2,0:T(8,128)S(1)}, f32[8,8,33,128]{3,1,2,0:T(8,128)}, u32[]{:S(2)}) copy-start(f32[8,8,33,128]{3,1,2,0:T(8,128)} %multiply_subtract_fusion.2) | copy-start | bytes 3244036
  102.9 1.9 %copy-start.7 = (f32[8,9,32,128]{3,1,2,0:T(8,128)S(1)}, f32[8,9,32,128]{3,1,2,0:T(8,128)}, u32[]{:S(2)}) copy-start(f32[8,9,32,128]{3,1,2,0:T(8,128)} %multiply_subtract_fusion) | copy-start | bytes 3538948
  102.9 2.2 %copy-start.20 = (f32[8,8,32,128]{3,2,1,0:T(8,128)S(1)}, f32[8,8,32,128]{3,2,1,0:T(8,128)}, u32[]{:S(2)}) copy-start(f32[8,8,32,128]{3,2,1,0:T(8,128)} %param.4) | copy-start | bytes 3145732
where the time goes:
time: 112 us; the launch traced here: 111 us
  other arithmetic  43.6 us (39%)
  blocking collectives  30.1 us (27%)
  local copies, waits for them, and re-layouts  27.7 us (25%)
  starting transfers between devices  7.7 us (7%)
  between operations  1.96 us (2%)
    all_gather x1, blocking collectives, on_device(): lax.all_gather(inner_src, 'gy', axis=3, tiled=True)  15.1 us
    all_gather x1, blocking collectives, on_device(): lax.all_gather(outer_src, 'gy', axis=3, tiled=True)  15 us
    unnamed x50, other arithmetic  14.1 us
    unnamed x58, local copies, waits for them, and re-layouts  14 us
    ppermute x2, starting transfers between devices, with_halo(): after = lax.ppermute(first, axis, down)  7.32 us
    sub x3, other arithmetic, rusanov(): 0.5 * (flux_left + flux_right) - 0.5 * speed * (cons_right - cons_left)  5.88 us
    add x1, other arithmetic, section_update(): return 0.5 * old + 0.5 * (conserved(core) + time_step * rates)  4.85 us
    add x3, other arithmetic, sweep(): left = take(padded, 1, length - 2) + 0.5 * take(slope, 0, length - 3)  3.84 us
  transfers between devices with their start and end apart: 4, of which 0 were waited for; matrix products, arithmetic and copies ran while one was open for 37% of the time, Pallas kernels for 0%

commit v1 on v0

--- a/solution.py
+++ b/solution.py
@@ -7,6 +7,20 @@
 omega_rate = 1.0
 shear_rate = 1.5
 time_step = 0.1
+
+
+def make_ranges_in(local_x):
+    parts_out, earlier = (lax.psum(1, axis_name="gy"), lax.axis_index("gy"))
+    everything, value_now = (local_x, 1)
+    while value_now < parts_out:
+        base_arr = lax.ppermute(
+            everything, axis_name="gy", perm=[(s, s ^ value_now) for s in range(parts_out)]
+        )
+        part_next = jnp.concatenate([everything, base_arr], 3)
+        u1 = jnp.concatenate([base_arr, everything], 3)
+        everything = jnp.where(earlier & value_now == 0, part_next, u1)
+        value_now = 2 * value_now
+    return everything
 
 
 def with_halo(shard, sides, width):
@@ -127,7 +141,7 @@
     inner_src = padded[:, :, 0:2, 2:-2]
     outer_src = padded[:, :, -2:, 2:-2]
     inner_cycle, outer_cycle = (
-        lax.all_gather(inner_src, "gy", axis=3, tiled=True),
+        make_ranges_in(inner_src),
         lax.all_gather(outer_src, "gy", axis=3, tiled=True),
     )
     position = lax.axis_index("gy") * cells

time: 112 us -> 97.7 us (0.87)
  blocking collectives: 30.1 us -> 22.1 us
  local copies, waits for them, and re-layouts: 27.7 us -> 19.9 us
  other arithmetic: 43.6 us -> 38.4 us
  starting transfers between devices: 7.7 us -> 12.5 us
  waiting for transfers between devices: 0.01 us -> 2.2 us
    all_gather x1 -> x0, blocking collectives: 15.1 us -> none  [on_device(): lax.all_gather(inner_src, 'gy', axis=3, tiled=True)]
    all_gather x1, blocking collectives: 15 us -> 22.1 us  [on_device(): lax.all_gather(outer_src, 'gy', axis=3, tiled=True)]
    unnamed x58 -> x42, local copies, waits for them, and re-layouts: 14 us -> 7.3 us
    ppermute x0 -> x3, starting transfers between devices: none -> 4.94 us  [make_ranges_in(): lax.ppermute(everything, axis_name='gy', perm=[(s, s ^ value_now) for s i...]
    ppermute x2, starting transfers between devices: 7.32 us -> 4.22 us  [with_halo(): after = lax.ppermute(first, axis, down)]
    another operation x4, local copies, waits for them, and re-layouts: 3.5 us -> 0.43 us  [conserved(): jnp.stack([rho, rho * prims[1], rho * prims[2], rho * prims[3], energy, p...]
    ppermute x2, starting transfers between devices: 0.39 us -> 3.37 us  [with_halo(): before = lax.ppermute(last, axis, up)]
    unnamed x50, other arithmetic: 14.1 us -> 11.5 us
  transfers between devices with their start and end apart: 4 -> 7, of which waited for: 0 -> 2; matrix products, arithmetic and copies ran while one was open for 37% -> 25% of each run, Pallas kernels for 0% -> 0%
where the time goes in v1:
time: 97.7 us; the launch traced here: 97.2 us
  other arithmetic  38.4 us (39%)
  blocking collectives  22.1 us (23%)
  local copies, waits for them, and re-layouts  19.9 us (20%)
  starting transfers between devices  12.5 us (13%)
  waiting for transfers between devices  2.2 us (2%)
  between operations  2.13 us (2%)
    all_gather x1, blocking collectives, on_device(): lax.all_gather(outer_src, 'gy', axis=3, tiled=True)  22.1 us
    unnamed x50, other arithmetic  11.5 us
    unnamed x42, local copies, waits for them, and re-layouts  7.3 us
    sub x3, other arithmetic, rusanov(): 0.5 * (flux_left + flux_right) - 0.5 * speed * (cons_right - cons_left)  5.4 us
    ppermute x3, starting transfers between devices, make_ranges_in(): lax.ppermute(everything, axis_name='gy', perm=[(s, s ^ value_now) for s i...  4.94 us
    ppermute x2, starting transfers between devices, with_halo(): after = lax.ppermute(first, axis, down)  4.22 us
    add x3, other arithmetic, sweep(): left = take(padded, 1, length - 2) + 0.5 * take(slope, 0, length - 3)  3.81 us
    slice x2, local copies, waits for them, and re-layouts, with_halo(): last = lax.slice_in_dim(shard, length - width, length, axis=dim)  3.62 us
  transfers between devices with their start and end apart: 7, of which 2 were waited for; matrix products, arithmetic and copies ran while one was open for 25% of the time, Pallas kernels for 0%

profile of v1, /device:TPU:0, one launch (start us, length us, event | category | flops | bytes accessed | tf_op | source)
XLA Modules:
  0.0 97.2 jit_solution(2512815240417189124)
XLA Ops:
  0.0 1.9 %copy.190 = f32[8,8,32,128]{3,1,2,0:T(8,128)S(1)} copy(f32[8,8,32,128]{3,2,1,0:T(8,128)} %param.5) | data formatting | bytes 2097152 | tf_op args[1]
  2.0 3.0 %collective-permute-start = (f32[8,8,2,128]{3,1,2,0:T(8,128)S(1)}, f32[8,8,2,128]{3,1,2,0:T(8,128)S(1)}, u32[]{:S(2)}, u32[]{:S(2)}) collective-permute-start(f32[8,8,2,128]{3,1,2,0:T(8,128)S(1)} %get-tuple-element.79), channel_id=1, source_target_pairs={{0,8},{8,16},{16,24},{24,0},{1,9},{9,17},{17,25},{25,1},{2,10},{10... | collective-permute-start | bytes 196616 | tf_op jit(solution)/shard_map/ppermute | solution.py:33
  4.9 1.0 %collective-permute-start.4 = (f32[8,8,2,128]{3,1,2,0:T(8,128)S(1)}, f32[8,8,2,128]{3,1,2,0:T(8,128)S(1)}, u32[]{:S(2)}, u32[]{:S(2)}) collective-permute-start(f32[8,8,2,128]{3,1,2,0:T(8,128)S(1)} %get-tuple-element.78), channel_id=1, source_target_pairs={{8,0},{16,8},{24,16},{0,24},{9,1},{17,9},{25,17},{1,25},{10,2},{18... | collective-permute-start | bytes 196616 | tf_op jit(solution)/shard_map/ppermute | solution.py:34
  6.9 2.1 %copy_subtract_fusion = f32[8,11,32,128]{3,1,2,0:T(8,128)S(1)} fusion(f32[8,11,32,128]{3,2,1,0:T(8,128)S(1)} %get-tuple-element.51, f32[8,11,32,128]{3,2,1,0:T(8,128)S(1)} %get-tuple-element.50), kind=kLoop, calls=%fused_computation.12 | loop fusion | flops 360448 | bytes 4325376 | tf_op jit(solution)/shard_map/sub | solution.py:98
  8.9 1.5 %minimum_multiply_fusion = f32[8,10,32,128]{3,1,2,0:T(8,128)S(1)} fusion(f32[8,11,32,128]{3,1,2,0:T(8,128)S(1)} %copy_subtract_fusion), kind=kLoop, calls=%fused_computation.14 | loop fusion | flops 2621440 | bytes 3932160 | tf_op jit(solution)/shard_map/mul | solution.py:77
  10.4 2.2 %fusion.1 = (f32[8,9,32,128]{3,1,2,0:T(8,128)S(1)}, f32[8,9,32,128]{3,1,2,0:T(8,128)S(1)}) fusion(f32[8,10,32,128]{3,1,2,0:T(8,128)S(1)} %minimum_multiply_fusion, f32[8,9,32,128]{3,2,1,0:T(8,128)S(1)} %get-tuple-element.80, f32[8,9,32,128]{3,2,1,0:T(8,128)S(1)} %get-tuple-element.81), kind=kLoop, calls=%fused_computation.4 | loop fusion | flops 1179648 | bytes 7077888 | tf_op jit(solution)/shard_map/add | solution.py:100
  15.3 1.9 %multiply_subtract_fusion = f32[8,9,32,128]{3,1,2,0:T(8,128)} fusion(f32[8,9,32,128]{3,1,2,0:T(8,128)S(1)} %get-tuple-element.89, f32[8,9,32,128]{3,1,2,0:T(8,128)S(1)} %get-tuple-element.88, f32[8,9,32,128]{3,1,2,0:T(8,128)S(1)} %get-tuple-element.45, f32[8,9,32,128]{3,1,2,0:T(8,128)S(1)} %get-tuple-element.43, f32[9,32,128]{2,0,1:T(8,128)S(1)} %get-tuple-element.19), kind=kLoop, calls=%fused_computation.13 | loop fusion | flops 1474560 | bytes 6045696 | tf_op jit(solution)/shard_map/sub | solution.py:88
  17.5 1.0 copy-done.10
  18.6 2.1 %collective-permute-start.2 = (f32[8,8,2,256]{3,1,2,0:T(8,128)S(1)}, f32[8,8,2,256]{3,1,2,0:T(8,128)}, u32[]{:S(2)}, u32[]{:S(2)}) collective-permute-start(f32[8,8,2,256]{3,1,2,0:T(8,128)S(1)} %maximum_select_fusion.2), channel_id=1, source_target_pairs={{0,2},{1,3},{2,0},{3,1},{4,6},{5,7},{6,4},{7,5},{8,10},{9,11},{10,... | collective-permute-start | bytes 393224 | tf_op jit(solution)/shard_map/ppermute | solution.py:16
  22.7 2.0 %collective-permute-done.2 = f32[8,8,2,256]{3,1,2,0:T(8,128)} collective-permute-done((f32[8,8,2,256]{3,1,2,0:T(8,128)S(1)}, f32[8,8,2,256]{3,1,2,0:T(8,128)}, u32[]{:S(2)}, u32[]{:S(2)}) %collective-permute-start.2) | collective-permute-done | bytes 131104 | tf_op jit(solution)/shard_map/ppermute | solution.py:16
  24.8 1.0 %maximum_select_fusion.1 = f32[8,8,2,512]{3,1,2,0:T(8,128)S(1)} fusion(f32[8,8,2,256]{3,1,2,0:T(8,128)} %collective-permute-done.2, f32[8,8,2,256]{3,1,2,0:T(8,128)S(1)} %maximum_select_fusion.2, pred[]{:T(512)S(6)} %eq.21), kind=kLoop, calls=%fused_computation.53 | loop fusion | flops 196608 | bytes 524289 | tf_op jit(solution)/shard_map/jit(_where)/select_n | solution.py:21
  25.8 2.8 %collective-permute-start.3 = (f32[8,8,2,512]{3,1,2,0:T(8,128)S(1)}, f32[8,8,2,512]{3,1,2,0:T(8,128)S(1)}, u32[]{:S(2)}, u32[]{:S(2)}) collective-permute-start(f32[8,8,2,512]{3,1,2,0:T(8,128)S(1)} %maximum_select_fusion.1), channel_id=1, source_target_pairs={{0,4},{1,5},{2,6},{3,7},{4,0},{5,1},{6,2},{7,3},{8,12},{9,13},{10,... | collective-permute-start | bytes 786440 | tf_op jit(solution)/shard_map/ppermute | solution.py:16
  28.6 22.1 %all_gather.3 = f32[8,8,2,1024]{3,1,2,0:T(8,128)S(1)} all-gather(f32[8,8,2,128]{3,1,2,0:T(8,128)S(1)} %collective-permute-done.4), channel_id=1, replica_groups=mesh['gx'=4,'gy'=8] {'gy'}, dimensions={3}, use_global_device_ids=true | all-gather | bytes 589824 | tf_op jit(solution)/shard_map/all_gather | solution.py:145
  52.6 0.8 copy-done.3
  53.5 1.0 %multiply_bitcast_fusion.2 = (f32[8,33,128]{2,0,1:T(8,128)S(1)}, f32[1,8,33,128]{3,1,2,0:T(8,128)S(1)}, f32[1,8,33,128]{3,1,2,0:T(8,128)S(1)}, f32[8,8,33,128]{3...) fusion(f32[8,8,33,128]{3,1,2,0:T(8,128)S(1)} %get-tuple-element.29, ...), kind=kLoop, calls=%fused_computation.180 | loop fusion | flops 1486845 | bytes 2433024 | tf_op jit(solution)/shard_map/mul | solution.py:88
  56.6 0.8 constant_dynamic-update-slice_fusion.16
  59.5 0.8 constant_dynamic-update-slice_fusion.8
  60.4 1.8 %fusion.21 = (f32[8,8,36,2]{3,1,2,0:T(8,128)}, f32[8,8,36,2]{3,1,2,0:T(8,128)}) fusion(f32[8,8,36,128]{3,1,2,0:T(8,128)S(1)} %get-tuple-element.87), kind=kLoop, calls=%fused_computation.208 | loop fusion | bytes 73728 | tf_op jit(solution)/shard_map/slice | solution.py:31
  62.2 1.8 %copy.196 = f32[8,8,36,2]{2,1,3,0:T(8,128)S(1)} copy(f32[8,8,36,2]{3,1,2,0:T(8,128)} %get-tuple-element.52) | data formatting | bytes 36864 | tf_op jit(solution)/shard_map/slice | solution.py:31
  64.4 2.4 %copy.198 = f32[8,8,36,2]{2,1,3,0:T(8,128)} copy(f32[8,8,36,2]{3,1,2,0:T(8,128)} %get-tuple-element.53) | data formatting | bytes 36864 | tf_op jit(solution)/shard_map/slice | solution.py:32
  66.8 3.2 %collective-permute-start.6 = (f32[8,8,36,2]{2,1,3,0:T(8,128)}, f32[8,8,36,2]{2,1,3,0:T(8,128)}, u32[]{:S(2)}, u32[]{:S(2)}) collective-permute-start(f32[8,8,36,2]{2,1,3,0:T(8,128)} %copy.198), channel_id=1, source_target_pairs={{1,0},{2,1},{3,2},{4,3},{5,4},{6,5},{7,6},{0,7},{9,8},{10,9},{11,1... | collective-permute-start | bytes 55304 | tf_op jit(solution)/shard_map/ppermute | solution.py:34
  70.0 0.7 constant_dynamic-update-slice_fusion.15
  70.7 0.7 constant_dynamic-update-slice_fusion.14
  71.5 0.7 constant_dynamic-update-slice_fusion.13
  75.1 2.9 %multiply_subtract_fusion.2 = f32[8,8,33,128]{3,1,2,0:T(8,128)} fusion(f32[8,8,33,128]{3,1,2,0:T(8,128)S(1)} %get-tuple-element.93, f32[8,8,33,128]{3,1,2,0:T(8,128)S(1)} %get-tuple-element.92, f32[8,8,33,128]{3,1,2,0:T(8,128)} %get-tuple-element.60, f32[8,8,33,128]{3,1,2,0:T(8,128)} %get-tuple-element.54, f32[8,33,128]{2,0,1:T(8,128)S(1)} %get-tuple-element.5), kind=kLoop, calls=%fused_computation.29 | loop fusion | flops 1351680 | bytes 5541888 | tf_op jit(solution)/shard_map/sub | solution.py:88
  78.0 1.4 %copy.197 = f32[8,8,36,2]{3,1,2,0:T(8,128)S(1)} copy(f32[8,8,36,2]{2,1,3,0:T(8,128)} %collective-permute-done.5) | data formatting | bytes 36864 | tf_op jit(solution)/shard_map/ppermute | solution.py:33
  79.4 2.4 %copy.200 = f32[8,8,36,2]{3,1,2,0:T(8,128)} copy(f32[8,8,36,2]{2,1,3,0:T(8,128)} %collective-permute-done.6) | data formatting | bytes 36864 | tf_op jit(solution)/shard_map/ppermute | solution.py:34
  81.8 2.2 %pad_maximum_fusion = f32[8,8,36,132]{3,1,2,0:T(8,128)S(1)} fusion(f32[8,8,36,2]{3,1,2,0:T(8,128)} %copy.200, f32[8,8,36,128]{3,1,2,0:T(8,128)S(1)} %get-tuple-element.87, f32[8,8,36,2]{3,1,2,0:T(8,128)S(1)} %copy.197), kind=kLoop, calls=%fused_computation | loop fusion | flops 608256 | bytes 2433024 | tf_op jit(solution)/shard_map/concatenate | solution.py:35
  84.7 1.4 %minimum_multiply_fusion.1 = f32[8,8,32,130]{3,1,2,0:T(8,128)S(1)} fusion(f32[8,8,32,131]{3,1,2,0:T(8,128)S(1)} %slice_subtract_fusion), kind=kLoop, calls=%fused_computation.16 | loop fusion | flops 2129920 | bytes 3194880 | tf_op jit(solution)/shard_map/mul | solution.py:77
  86.2 1.5 %fusion.3 = (f32[8,8,32,129]{3,1,2,0:T(8,128)S(1)}, f32[8,8,32,129]{3,1,2,0:T(8,128)S(1)}) fusion(f32[8,8,32,130]{3,1,2,0:T(8,128)S(1)} %minimum_multiply_fusion.1, f32[8,8,36,128]{3,1,2,0:T(8,128)S(1)} %get-tuple-element.87, f32[8,8,36,2]{3,1,2,0:T(8,128)S(1)} %copy.197, f32[8,8,36,2]{3,1,2,0:T(8,128)S(1)} %copy-done.1), kind=kLoop, calls=%fused_computation.9 | loop fusion | flops 1585152 | bytes 5443584 | tf_op jit(solution)/shard_map/add | solution.py:100
  92.9 3.2 %fusion.12 = f32[8,8,32,128]{3,1,2,0:T(8,128)S(1)} fusion(f32[8,9,32,128]{3,1,2,0:T(8,128)S(1)} %copy-done.5, f32[8,8,32,129]{3,1,2,0:T(8,128)S(1)} %multiply_subtract_fusion.1, f32[8,8,33,128]{3,1,2,0:T(8,128)S(1)} %copy-done.4, f32[8,8,32,128]{3,2,1,0:T(8,128)S(1)} %copy-done.12, f32[8,8,32,128]{3,2,1,0:T(8,128)S(1)} %copy-done.9, ...), kind=kLoop, calls=%fused_computation.37 | loop fusion | flops 2883584 | bytes 10485760 | tf_op jit(solution)/shard_map/add | solution.py:130
  96.1 1.2 %copy.209 = f32[8,8,32,128]{3,2,1,0:T(8,128)} copy(f32[8,8,32,128]{3,1,2,0:T(8,128)S(1)} %fusion.12) | data formatting | bytes 2097152 | tf_op jit(solution)/shard_map/add | solution.py:130
  (124 shorter events, 19.3 us)
Async XLA Ops:
  0.0 6.0 %copy-start = (f32[8,8,32,128]{3,2,1,0:T(8,128)S(1)}, f32[8,8,32,128]{3,2,1,0:T(8,128)}, u32[]{:S(2)}) copy-start(f32[8,8,32,128]{3,2,1,0:T(8,128)} %param.5) | copy-start | bytes 3145732
  1.9 50.0 %copy-start.2 = (f32[8,8,32,128]{3,1,2,0:T(8,128)}, f32[8,8,32,128]{3,1,2,0:T(8,128)S(1)}, u32[]{:S(2)}) copy-start(f32[8,8,32,128]{3,1,2,0:T(8,128)S(1)} %copy.190) | copy-start | bytes 3145732
  2.0 15.3 %collective-permute-start = (f32[8,8,2,128]{3,1,2,0:T(8,128)S(1)}, f32[8,8,2,128]{3,1,2,0:T(8,128)S(1)}, u32[]{:S(2)}, u32[]{:S(2)}) collective-permute-start(f32[8,8,2,128]{3,1,2,0:T(8,128)S(1)} %get-tuple-element.79), channel_id=1, source_target_pairs={{0,8},{8,16},{16,24},{24,0},{1,9},{9,17},{17,25},{25,1},{2,10},{10... | collective-permute-start | bytes 196616 | tf_op jit(solution)/shard_map/ppermute | solution.py:33
  4.9 23.7 %collective-permute-start.4 = (f32[8,8,2,128]{3,1,2,0:T(8,128)S(1)}, f32[8,8,2,128]{3,1,2,0:T(8,128)S(1)}, u32[]{:S(2)}, u32[]{:S(2)}) collective-permute-start(f32[8,8,2,128]{3,1,2,0:T(8,128)S(1)} %get-tuple-element.78), channel_id=1, source_target_pairs={{8,0},{16,8},{24,16},{0,24},{9,1},{17,9},{25,17},{1,25},{10,2},{18... | collective-permute-start | bytes 196616 | tf_op jit(solution)/shard_map/ppermute | solution.py:34
  17.3 1.3 %collective-permute-start.1 = (f32[8,8,2,128]{3,1,2,0:T(8,128)S(1)}, f32[8,8,2,128]{3,1,2,0:T(8,128)S(1)}, u32[]{:S(2)}, u32[]{:S(2)}) collective-permute-start(f32[8,8,2,128]{3,1,2,0:T(8,128)S(1)} %collective-permute-done), channel_id=1, source_target_pairs={{0,1},{1,0},{2,3},{3,2},{4,5},{5,4},{6,7},{7,6},{8,9},{9,8},{10,11... | collective-permute-start | bytes 196616 | tf_op jit(solution)/shard_map/ppermute | solution.py:16
  17.5 1.0 copy-start.10
  18.6 6.2 %collective-permute-start.2 = (f32[8,8,2,256]{3,1,2,0:T(8,128)S(1)}, f32[8,8,2,256]{3,1,2,0:T(8,128)}, u32[]{:S(2)}, u32[]{:S(2)}) collective-permute-start(f32[8,8,2,256]{3,1,2,0:T(8,128)S(1)} %maximum_select_fusion.2), channel_id=1, source_target_pairs={{0,2},{1,3},{2,0},{3,1},{4,6},{5,7},{6,4},{7,5},{8,10},{9,11},{10,... | collective-permute-start | bytes 393224 | tf_op jit(solution)/shard_map/ppermute | solution.py:16
  20.7 30.4 %copy-start.8 = (f32[8,8,32,128]{3,2,1,0:T(8,128)}, f32[8,8,32,128]{3,2,1,0:T(8,128)S(1)}, u32[]{:S(2)}) copy-start(f32[8,8,32,128]{3,2,1,0:T(8,128)S(1)} %slice_dynamic-update-slice_fusion.6) | copy-start | bytes 3145732
  25.8 25.1 %collective-permute-start.3 = (f32[8,8,2,512]{3,1,2,0:T(8,128)S(1)}, f32[8,8,2,512]{3,1,2,0:T(8,128)S(1)}, u32[]{:S(2)}, u32[]{:S(2)}) collective-permute-start(f32[8,8,2,512]{3,1,2,0:T(8,128)S(1)} %maximum_select_fusion.1), channel_id=1, source_target_pairs={{0,4},{1,5},{2,6},{3,7},{4,0},{5,1},{6,2},{7,3},{8,12},{9,13},{10,... | collective-permute-start | bytes 786440 | tf_op jit(solution)/shard_map/ppermute | solution.py:16
  52.1 1.2 %copy-start.3 = (f32[8,8,32,128]{3,1,2,0:T(8,128)S(1)}, f32[8,8,32,128]{3,1,2,0:T(8,128)}, u32[]{:S(2)}) copy-start(f32[8,8,32,128]{3,1,2,0:T(8,128)} %copy-done.2) | copy-start | bytes 3145732
  64.0 14.0 %collective-permute-start.5 = (f32[8,8,36,2]{2,1,3,0:T(8,128)S(1)}, f32[8,8,36,2]{2,1,3,0:T(8,128)}, u32[]{:S(2)}, u32[]{:S(2)}) collective-permute-start(f32[8,8,36,2]{2,1,3,0:T(8,128)S(1)} %copy.196), channel_id=1, source_target_pairs={{0,1},{1,2},{2,3},{3,4},{4,5},{5,6},{6,7},{7,0},{8,9},{9,10},{10,1... | collective-permute-start | bytes 55304 | tf_op jit(solution)/shard_map/ppermute | solution.py:33
  66.8 5.4 %copy-start.14 = (f32[1,8,33,128]{3,1,2,0:T(8,128)S(1)}, f32[1,8,33,128]{3,1,2,0:T(8,128)}, u32[]{:S(2)}) copy-start(f32[1,8,33,128]{3,1,2,0:T(8,128)} %get-tuple-element.9) | copy-start | bytes 405508
  66.8 6.1 %copy-start.6 = (f32[8,8,33,128]{3,1,2,0:T(8,128)S(1)}, f32[8,8,33,128]{3,1,2,0:T(8,128)}, u32[]{:S(2)}) copy-start(f32[8,8,33,128]{3,1,2,0:T(8,128)} %get-tuple-element.66) | copy-start | bytes 3244036
  66.8 12.6 %collective-permute-start.6 = (f32[8,8,36,2]{2,1,3,0:T(8,128)}, f32[8,8,36,2]{2,1,3,0:T(8,128)}, u32[]{:S(2)}, u32[]{:S(2)}) collective-permute-start(f32[8,8,36,2]{2,1,3,0:T(8,128)} %copy.198), channel_id=1, source_target_pairs={{1,0},{2,1},{3,2},{4,3},{5,4},{6,5},{7,6},{0,7},{9,8},{10,9},{11,1... | collective-permute-start | bytes 55304 | tf_op jit(solution)/shard_map/ppermute | solution.py:34
  71.5 3.5 %copy-start.13 = (f32[1,8,33,128]{3,1,2,0:T(8,128)S(1)}, f32[1,8,33,128]{3,1,2,0:T(8,128)}, u32[]{:S(2)}) copy-start(f32[1,8,33,128]{3,1,2,0:T(8,128)} %get-tuple-element.11) | copy-start | bytes 405508
  72.9 2.1 %copy-start.7 = (f32[8,8,33,128]{3,1,2,0:T(8,128)S(1)}, f32[8,8,33,128]{3,1,2,0:T(8,128)}, u32[]{:S(2)}) copy-start(f32[8,8,33,128]{3,1,2,0:T(8,128)} %constant_dynamic-update-slice_fusion.21) | copy-start | bytes 3244036
  84.7 1.5 %copy-start.1 = (f32[8,8,36,2]{3,1,2,0:T(8,128)S(1)}, f32[8,8,36,2]{3,1,2,0:T(8,128)}, u32[]{:S(2)}) copy-start(f32[8,8,36,2]{3,1,2,0:T(8,128)} %copy.200) | copy-start | bytes 55300
  90.0 1.2 %copy-start.4 = (f32[8,8,33,128]{3,1,2,0:T(8,128)S(1)}, f32[8,8,33,128]{3,1,2,0:T(8,128)}, u32[]{:S(2)}) copy-start(f32[8,8,33,128]{3,1,2,0:T(8,128)} %multiply_subtract_fusion.2) | copy-start | bytes 3244036
  90.1 1.9 %copy-start.5 = (f32[8,9,32,128]{3,1,2,0:T(8,128)S(1)}, f32[8,9,32,128]{3,1,2,0:T(8,128)}, u32[]{:S(2)}) copy-start(f32[8,9,32,128]{3,1,2,0:T(8,128)} %multiply_subtract_fusion) | copy-start | bytes 3538948
  90.1 2.2 %copy-start.9 = (f32[8,8,32,128]{3,2,1,0:T(8,128)S(1)}, f32[8,8,32,128]{3,2,1,0:T(8,128)}, u32[]{:S(2)}) copy-start(f32[8,8,32,128]{3,2,1,0:T(8,128)} %copy-done.8) | copy-start | bytes 3145732
  90.1 2.5 %copy-start.11 = (f32[8,8,32,128]{3,2,1,0:T(8,128)S(1)}, f32[8,8,32,128]{3,2,1,0:T(8,128)}, u32[]{:S(2)}) copy-start(f32[8,8,32,128]{3,2,1,0:T(8,128)} %constant_dynamic-update-slice_fusion.58) | copy-start | bytes 3145732
  90.1 2.8 %copy-start.12 = (f32[8,8,32,128]{3,2,1,0:T(8,128)S(1)}, f32[8,8,32,128]{3,2,1,0:T(8,128)}, u32[]{:S(2)}) copy-start(f32[8,8,32,128]{3,2,1,0:T(8,128)} %param.4) | copy-start | bytes 3145732
